TPU v7x, 32 devices: a whole 2x2x4 slice. The times are simulated.
32 devices in a mesh: group: 2 (over y), row: 8 (over z, x), col: 2 (over core).
Axes of the slice: x: 2, y: 2, z: 4, core: 2. Of those that a mesh axis runs over, the one named last changes fastest.
Arguments:
- map_in: bfloat16 [192, 96, 48], P(('group', 'row'), 'col'), parts along dimension 0, may hold values from -6 to 6
- embedding: bfloat16 [192, 96], P(('group', 'row')), parts along dimension 0, may hold values from -6 to 6
- w_row: bfloat16 [96, 48], replicated, may hold values from -0.625 to 0.625
- w_col: bfloat16 [96, 48], replicated, may hold values from -0.625 to 0.625
- first_kernel_weight: bfloat16 [3, 3, 48, 48], replicated, may hold values from -0.3125 to 0.3125
- first_bias: float32 [48], replicated, may hold values from -0.5 to 0.5
- second_kernel_weight: bfloat16 [3, 3, 48, 48], replicated, may hold values from -0.3125 to 0.3125
- second_bias: float32 [48], replicated, may hold values from -0.5 to 0.5
- w_mix: bfloat16 [48, 48], replicated, may hold values from -0.875 to 0.875
- b_mix: float32 [48], replicated, may hold values from -0.5 to 0.5
- w_head: float32 [48], replicated, may hold values from -0.875 to 0.875
Outputs:
- contacts: float32 [192, 96], P(('group', 'row'), 'col'), parts along dimension 0
There are 2 independent parts, one for each index of `group`. A program takes and returns all parts, laid end to end along the dimension named above; an argument that names none is the same for every part. Nothing has to cross between parts.
All inputs are finite; a program needn't handle non-finite values.
Results may differ from a plain program's by a relative error of at most 0.0055.
Values may be sent and summed in bfloat16 or wider, within the bound.
A program may use at most 64 MiB of HBM per device.

v0:
```python
import jax
import jax.numpy as jnp
from jax import lax
from jax.sharding import PartitionSpec as P

FIRST_DILATION = 4
SECOND_DILATION = 8


def padded(array, sides, width):
    for axis, dim in sides:
        peers, length = (lax.axis_size(axis), array.shape[dim])
        up = [(i, (i + 1) % peers) for i in range(peers - 1)]
        down = [(j, i) for i, j in up]
        last = lax.slice_in_dim(array, length - width, length, axis=dim)
        leading = lax.slice_in_dim(array, 0, width, axis=dim)
        before = lax.ppermute(last, axis, up)
        after = lax.ppermute(leading, axis, down)
        array = jnp.concatenate([before, array, after], axis=dim)
    return array


def swapped(value, axis, bit):
    mask = 2**bit
    pairs = [(source, source ^ mask) for source in range(lax.axis_size(axis))]
    return lax.ppermute(value, axis, pairs)


def dilated_conv(active, weight, spacing, out_rows, out_cols):
    windows = []
    for tap_row in range(3):
        for tap_col in range(3):
            windows.append(
                active[
                    tap_row * spacing : tap_row * spacing + out_rows,
                    tap_col * spacing : tap_col * spacing + out_cols,
                ]
            )
    stacked = jnp.concatenate(windows, axis=-1)
    flat_weight = weight.reshape(9 * weight.shape[2], weight.shape[3])
    return jnp.einsum("rch,hk->rck", stacked, flat_weight, preferred_element_type=jnp.float32)


def on_device(
    map_in,
    embedding,
    w_row,
    w_col,
    first_kernel_weight,
    first_bias,
    second_kernel_weight,
    second_bias,
    w_mix,
    b_mix,
    w_head,
):
    patch_rows, patch_columns, channels = map_in.shape
    row_count = lax.axis_size("row")
    row_at = lax.axis_index("row")
    col_at = lax.axis_index("col")
    all_bins = lax.all_gather(embedding, "row", axis=0, tiled=True)
    row_terms = jnp.dot(all_bins, w_row, preferred_element_type=jnp.float32)
    col_terms = jnp.dot(all_bins, w_col, preferred_element_type=jnp.float32)
    own_rows = lax.dynamic_slice_in_dim(row_terms, row_at * patch_rows, patch_rows, 0)
    own_cols = lax.dynamic_slice_in_dim(col_terms, col_at * patch_columns, patch_columns, 0)
    contact_grid = (
        map_in.astype(jnp.float32) + own_rows[:, None, :] + own_cols[None, :, :]
    ).astype(jnp.bfloat16)
    first_padded = padded(contact_grid, (("row", 0), ("col", 1)), FIRST_DILATION)
    first_layer = (
        contact_grid.astype(jnp.float32)
        + dilated_conv(
            jnp.maximum(first_padded, 0),
            first_kernel_weight,
            FIRST_DILATION,
            patch_rows,
            patch_columns,
        )
        + first_bias
    ).astype(jnp.bfloat16)
    second_padded = padded(first_layer, (("row", 0), ("col", 1)), SECOND_DILATION)
    second_layer = (
        first_layer.astype(jnp.float32)
        + dilated_conv(
            jnp.maximum(second_padded, 0),
            second_kernel_weight,
            SECOND_DILATION,
            patch_rows,
            patch_columns,
        )
        + second_bias
    ).astype(jnp.bfloat16)
    half_rows = patch_rows // 2
    blocks_per = row_count // 2
    arranged = second_layer.reshape(2, half_rows, blocks_per, patch_rows, channels)
    arranged = arranged.transpose(0, 2, 1, 3, 4).reshape(
        2 * blocks_per, half_rows, patch_rows, channels
    )
    exchanged = lax.all_to_all(
        lax.all_to_all(arranged, "row", split_axis=0, concat_axis=0, tiled=True),
        "col",
        split_axis=0,
        concat_axis=0,
        tiled=True,
    )
    exchanged = exchanged.reshape(2, blocks_per, half_rows, patch_rows, channels)
    top_half = row_at // blocks_per
    kept_part = lax.dynamic_index_in_dim(exchanged, top_half, 0, keepdims=False)
    sent_part = lax.dynamic_index_in_dim(exchanged, 1 - top_half, 0, keepdims=False)
    came_back = swapped(sent_part, "row", blocks_per.bit_length() - 1)
    stacked = jnp.where(
        top_half == 0, jnp.stack([kept_part, came_back]), jnp.stack([came_back, kept_part])
    )
    mirrored = stacked.transpose(3, 1, 0, 2, 4).reshape(patch_rows, patch_columns, channels)
    symmetric = ((second_layer.astype(jnp.float32) + mirrored.astype(jnp.float32)) * 0.5).astype(
        jnp.bfloat16
    )
    mixture = (
        jnp.einsum("rch,hk->rck", symmetric, w_mix, preferred_element_type=jnp.float32) + b_mix
    )
    mixture = jnp.maximum(mixture, 0.0)
    return jnp.sum(mixture * w_head, axis=-1)


def solution(mesh):
    placed = (
        P(("group", "row"), "col", None),
        P(("group", "row"), None),
        P(),
        P(),
        P(),
        P(),
        P(),
        P(),
        P(),
        P(),
        P(),
    )
    return jax.shard_map(
        on_device, mesh=mesh, in_specs=placed, out_specs=P(("group", "row"), "col"), check_vma=False
    )
```

profile of v0, /device:TPU:0, one launch (start us, length us, event | category | flops | bytes accessed | tf_op | source)
XLA Modules:
  0.0 92.6 jit_solution(15328792908924847365)
XLA Ops:
  0.0 0.7 copy-done.5
  0.7 32.3 %all-gather = bf16[8,12,96]{2,1,0:T(8,128)(2,1)S(1)} all-gather(bf16[1,12,96]{2,1,0:T(8,128)(2,1)S(1)} %bitcast.32), channel_id=1, replica_groups=mesh['group'=2,'row'=8,'col'=2] {'row'}, dimensions={0}, use_global_device_ids=true | all-gather | bytes 20736 | tf_op jit(solution)/shard_map/all_gather | solution.py:61
  34.0 3.4 %collective-permute-start = (bf16[4,48,48]{2,1,0:T(8,128)(2,1)S(1)}, bf16[4,48,48]{2,1,0:T(8,128)(2,1)S(1)}, u32[]{:S(2)}, u32[]{:S(2)}) collective-permute-start(bf16[4,48,48]{2,1,0:T(8,128)(2,1)S(1)} %get-tuple-element.31), channel_id=1, source_target_pairs={{0,2},{2,4},{4,6},{6,8},{8,10},{10,12},{12,14},{1,3},{3,5},{5,7},{... | collective-permute-start | bytes 55304 | tf_op jit(solution)/shard_map/ppermute | solution.py:17
  37.4 1.3 %collective-permute-start.1 = (bf16[4,48,48]{2,1,0:T(8,128)(2,1)S(1)}, bf16[4,48,48]{2,1,0:T(8,128)(2,1)S(1)}, u32[]{:S(2)}, u32[]{:S(2)}) collective-permute-start(bf16[4,48,48]{2,1,0:T(8,128)(2,1)S(1)} %get-tuple-element.32), channel_id=1, source_target_pairs={{2,0},{4,2},{6,4},{8,6},{10,8},{12,10},{14,12},{3,1},{5,3},{7,5},{... | collective-permute-start | bytes 55304 | tf_op jit(solution)/shard_map/ppermute | solution.py:18
  39.2 4.3 %collective-permute-done.1 = bf16[4,48,48]{2,1,0:T(8,128)(2,1)S(1)} collective-permute-done((bf16[4,48,48]{2,1,0:T(8,128)(2,1)S(1)}, bf16[4,48,48]{2,1,0:T(8,128)(2,1)S(1)}, u32[]{:S(2)}, u32[]{:S(2)}) %collective-permute-start.1) | collective-permute-done | bytes 18464 | tf_op jit(solution)/shard_map/ppermute | solution.py:18
  43.4 1.3 %collective-permute-start.2 = (bf16[20,4,48]{2,1,0:T(4,128)(2,1)S(1)}, bf16[20,4,48]{2,1,0:T(4,128)(2,1)S(1)}, u32[]{:S(2)}, u32[]{:S(2)}) collective-permute-start(bf16[20,4,48]{2,1,0:T(4,128)(2,1)S(1)} %get-tuple-element.25), channel_id=1, source_target_pairs={{0,1},{2,3},{4,5},{6,7},{8,9},{10,11},{12,13},{14,15},{16,17},{18,... | collective-permute-start | bytes 23048 | tf_op jit(solution)/shard_map/ppermute | solution.py:17
  44.7 1.3 %collective-permute-start.3 = (bf16[20,4,48]{2,1,0:T(4,128)(2,1)S(1)}, bf16[20,4,48]{2,1,0:T(4,128)(2,1)S(1)}, u32[]{:S(2)}, u32[]{:S(2)}) collective-permute-start(bf16[20,4,48]{2,1,0:T(4,128)(2,1)S(1)} %get-tuple-element.26), channel_id=1, source_target_pairs={{1,0},{3,2},{5,4},{7,6},{9,8},{11,10},{13,12},{15,14},{17,16},{19,... | collective-permute-start | bytes 23048 | tf_op jit(solution)/shard_map/ppermute | solution.py:18
  46.0 1.8 %collective-permute-done.3 = bf16[20,4,48]{2,1,0:T(4,128)(2,1)S(1)} collective-permute-done((bf16[20,4,48]{2,1,0:T(4,128)(2,1)S(1)}, bf16[20,4,48]{2,1,0:T(4,128)(2,1)S(1)}, u32[]{:S(2)}, u32[]{:S(2)}) %collective-permute-start.3) | collective-permute-done | bytes 7712 | tf_op jit(solution)/shard_map/ppermute | solution.py:18
  48.2 0.6 concatenate.20
  48.8 0.6 copy-done.6
  49.8 2.8 %collective-permute-start.4 = (bf16[8,48,48]{2,1,0:T(8,128)(2,1)S(1)}, bf16[8,48,48]{2,1,0:T(8,128)(2,1)S(1)}, u32[]{:S(2)}, u32[]{:S(2)}) collective-permute-start(bf16[8,48,48]{2,1,0:T(8,128)(2,1)S(1)} %get-tuple-element.29), channel_id=1, source_target_pairs={{0,2},{2,4},{4,6},{6,8},{8,10},{10,12},{12,14},{1,3},{3,5},{5,7},{... | collective-permute-start | bytes 110600 | tf_op jit(solution)/shard_map/ppermute | solution.py:17
  52.7 1.3 %collective-permute-start.5 = (bf16[8,48,48]{2,1,0:T(8,128)(2,1)S(1)}, bf16[8,48,48]{2,1,0:T(8,128)(2,1)S(1)}, u32[]{:S(2)}, u32[]{:S(2)}) collective-permute-start(bf16[8,48,48]{2,1,0:T(8,128)(2,1)S(1)} %get-tuple-element.30), channel_id=1, source_target_pairs={{2,0},{4,2},{6,4},{8,6},{10,8},{12,10},{14,12},{3,1},{5,3},{7,5},{... | collective-permute-start | bytes 110600 | tf_op jit(solution)/shard_map/ppermute | solution.py:18
  54.0 1.1 %collective-permute-done.4 = bf16[8,48,48]{2,1,0:T(8,128)(2,1)S(1)} collective-permute-done((bf16[8,48,48]{2,1,0:T(8,128)(2,1)S(1)}, bf16[8,48,48]{2,1,0:T(8,128)(2,1)S(1)}, u32[]{:S(2)}, u32[]{:S(2)}) %collective-permute-start.4) | collective-permute-done | bytes 36896 | tf_op jit(solution)/shard_map/ppermute | solution.py:17
  55.0 4.2 %collective-permute-done.5 = bf16[8,48,48]{2,1,0:T(8,128)(2,1)S(1)} collective-permute-done((bf16[8,48,48]{2,1,0:T(8,128)(2,1)S(1)}, bf16[8,48,48]{2,1,0:T(8,128)(2,1)S(1)}, u32[]{:S(2)}, u32[]{:S(2)}) %collective-permute-start.5) | collective-permute-done | bytes 36896 | tf_op jit(solution)/shard_map/ppermute | solution.py:18
  59.2 1.3 %collective-permute-start.6 = (bf16[28,8,48]{2,1,0:T(8,128)(2,1)S(1)}, bf16[28,8,48]{2,1,0:T(8,128)(2,1)S(1)}, u32[]{:S(2)}, u32[]{:S(2)}) collective-permute-start(bf16[28,8,48]{2,1,0:T(8,128)(2,1)S(1)} %get-tuple-element.14), channel_id=1, source_target_pairs={{0,1},{2,3},{4,5},{6,7},{8,9},{10,11},{12,13},{14,15},{16,17},{18,... | collective-permute-start | bytes 64520 | tf_op jit(solution)/shard_map/ppermute | solution.py:17
  60.5 1.3 %collective-permute-start.7 = (bf16[28,8,48]{2,1,0:T(8,128)(2,1)S(1)}, bf16[28,8,48]{2,1,0:T(8,128)(2,1)S(1)}, u32[]{:S(2)}, u32[]{:S(2)}) collective-permute-start(bf16[28,8,48]{2,1,0:T(8,128)(2,1)S(1)} %get-tuple-element.15), channel_id=1, source_target_pairs={{1,0},{3,2},{5,4},{7,6},{9,8},{11,10},{13,12},{15,14},{17,16},{19,... | collective-permute-start | bytes 64520 | tf_op jit(solution)/shard_map/ppermute | solution.py:18
  61.8 1.8 %collective-permute-done.7 = bf16[28,8,48]{2,1,0:T(8,128)(2,1)S(1)} collective-permute-done((bf16[28,8,48]{2,1,0:T(8,128)(2,1)S(1)}, bf16[28,8,48]{2,1,0:T(8,128)(2,1)S(1)}, u32[]{:S(2)}, u32[]{:S(2)}) %collective-permute-start.7) | collective-permute-done | bytes 21536 | tf_op jit(solution)/shard_map/ppermute | solution.py:18
  64.0 0.6 concatenate.23
  65.8 0.8 reshape.35
  66.6 6.0 %all-to-all-start = ((bf16[8,2,1728]{2,1,0:T(2,128)(2,1)}), bf16[8,2,1728]{2,1,0:T(2,128)(2,1)S(1)}, u32[]{:S(2)}, u32[]{:S(2)}) async-start(bf16[8,2,1728]{2,1,0:T(2,128)(2,1)} %reshape.35), calls=%async_computation | async-start | bytes 114688 | tf_op jit(solution)/shard_map/all_to_all | solution.py:100
  72.6 6.8 %all-to-all-done = bf16[8,2,1728]{2,1,0:T(2,128)(2,1)S(1)} async-done(((bf16[8,2,1728]{2,1,0:T(2,128)(2,1)}), bf16[8,2,1728]{2,1,0:T(2,128)(2,1)S(1)}, u32[]{:S(2)}, u32[]{:S(2)}) %all-to-all-start) | async-done | bytes 55328 | tf_op jit(solution)/shard_map/all_to_all | solution.py:100
  79.9 3.8 %all_to_all.10 = bf16[2,2,6912]{2,1,0:T(2,128)(2,1)S(1)} all-to-all(bf16[2,2,6912]{2,1,0:T(2,128)(2,1)S(1)} %reshape.37), channel_id=1, replica_groups=mesh['group'=2,'row'=8,'col'=2] {'col'}, dimensions={0} | all-to-all | bytes 110592 | tf_op jit(solution)/shard_map/all_to_all | solution.py:99
  84.6 6.0 %collective-permute-done.8 = bf16[4,6,12,48]{3,0,2,1:T(4,128)(2,1)S(1)} collective-permute-done((bf16[4,6,12,48]{3,0,2,1:T(4,128)(2,1)S(1)}, bf16[4,6,12,48]{3,0,2,1:T(4,128)(2,1)S(1)}, u32[]{:S(2)}, u32[]{:S(2)}) %collective-permute-start.8) | collective-permute-done | bytes 27680 | tf_op jit(solution)/shard_map/ppermute | solution.py:26
  91.7 0.9 fusion.6
  (51 shorter events, 5.9 us)
Async XLA Ops:
  0.0 48.8 %copy-start = (bf16[3,3,48,48]{3,2,1,0:T(8,128)(2,1)S(1)}, bf16[3,3,48,48]{3,2,1,0:T(8,128)(2,1)}, u32[]{:S(2)}) copy-start(bf16[3,3,48,48]{3,2,1,0:T(8,128)(2,1)} %param.15) | copy-start | bytes 124420
  0.0 0.7 copy-start.5
  0.7 32.3 %copy-start.3 = (bf16[96,48]{0,1:T(8,128)(2,1)S(1)}, bf16[96,48]{0,1:T(8,128)(2,1)}, u32[]{:S(2)}) copy-start(bf16[96,48]{0,1:T(8,128)(2,1)} %param.13) | copy-start | bytes 27652
  0.7 32.5 %copy-start.4 = (bf16[96,48]{0,1:T(8,128)(2,1)S(1)}, bf16[96,48]{0,1:T(8,128)(2,1)}, u32[]{:S(2)}) copy-start(bf16[96,48]{0,1:T(8,128)(2,1)} %param.14) | copy-start | bytes 27652
  33.0 0.9 copy-start.1
  34.0 5.1 %collective-permute-start = (bf16[4,48,48]{2,1,0:T(8,128)(2,1)S(1)}, bf16[4,48,48]{2,1,0:T(8,128)(2,1)S(1)}, u32[]{:S(2)}, u32[]{:S(2)}) collective-permute-start(bf16[4,48,48]{2,1,0:T(8,128)(2,1)S(1)} %get-tuple-element.31), channel_id=1, source_target_pairs={{0,2},{2,4},{4,6},{6,8},{8,10},{10,12},{12,14},{1,3},{3,5},{5,7},{... | collective-permute-start | bytes 55304 | tf_op jit(solution)/shard_map/ppermute | solution.py:17
  37.4 6.0 %collective-permute-start.1 = (bf16[4,48,48]{2,1,0:T(8,128)(2,1)S(1)}, bf16[4,48,48]{2,1,0:T(8,128)(2,1)S(1)}, u32[]{:S(2)}, u32[]{:S(2)}) collective-permute-start(bf16[4,48,48]{2,1,0:T(8,128)(2,1)S(1)} %get-tuple-element.32), channel_id=1, source_target_pairs={{2,0},{4,2},{6,4},{8,6},{10,8},{12,10},{14,12},{3,1},{5,3},{7,5},{... | collective-permute-start | bytes 55304 | tf_op jit(solution)/shard_map/ppermute | solution.py:18
  43.4 2.6 %collective-permute-start.2 = (bf16[20,4,48]{2,1,0:T(4,128)(2,1)S(1)}, bf16[20,4,48]{2,1,0:T(4,128)(2,1)S(1)}, u32[]{:S(2)}, u32[]{:S(2)}) collective-permute-start(bf16[20,4,48]{2,1,0:T(4,128)(2,1)S(1)} %get-tuple-element.25), channel_id=1, source_target_pairs={{0,1},{2,3},{4,5},{6,7},{8,9},{10,11},{12,13},{14,15},{16,17},{18,... | collective-permute-start | bytes 23048 | tf_op jit(solution)/shard_map/ppermute | solution.py:17
  44.7 3.1 %collective-permute-start.3 = (bf16[20,4,48]{2,1,0:T(4,128)(2,1)S(1)}, bf16[20,4,48]{2,1,0:T(4,128)(2,1)S(1)}, u32[]{:S(2)}, u32[]{:S(2)}) collective-permute-start(bf16[20,4,48]{2,1,0:T(4,128)(2,1)S(1)} %get-tuple-element.26), channel_id=1, source_target_pairs={{1,0},{3,2},{5,4},{7,6},{9,8},{11,10},{13,12},{15,14},{17,16},{19,... | collective-permute-start | bytes 23048 | tf_op jit(solution)/shard_map/ppermute | solution.py:18
  48.8 0.7 copy-start.6
  49.8 5.2 %collective-permute-start.4 = (bf16[8,48,48]{2,1,0:T(8,128)(2,1)S(1)}, bf16[8,48,48]{2,1,0:T(8,128)(2,1)S(1)}, u32[]{:S(2)}, u32[]{:S(2)}) collective-permute-start(bf16[8,48,48]{2,1,0:T(8,128)(2,1)S(1)} %get-tuple-element.29), channel_id=1, source_target_pairs={{0,2},{2,4},{4,6},{6,8},{8,10},{10,12},{12,14},{1,3},{3,5},{5,7},{... | collective-permute-start | bytes 110600 | tf_op jit(solution)/shard_map/ppermute | solution.py:17
  52.7 6.5 %collective-permute-start.5 = (bf16[8,48,48]{2,1,0:T(8,128)(2,1)S(1)}, bf16[8,48,48]{2,1,0:T(8,128)(2,1)S(1)}, u32[]{:S(2)}, u32[]{:S(2)}) collective-permute-start(bf16[8,48,48]{2,1,0:T(8,128)(2,1)S(1)} %get-tuple-element.30), channel_id=1, source_target_pairs={{2,0},{4,2},{6,4},{8,6},{10,8},{12,10},{14,12},{3,1},{5,3},{7,5},{... | collective-permute-start | bytes 110600 | tf_op jit(solution)/shard_map/ppermute | solution.py:18
  59.2 2.6 %collective-permute-start.6 = (bf16[28,8,48]{2,1,0:T(8,128)(2,1)S(1)}, bf16[28,8,48]{2,1,0:T(8,128)(2,1)S(1)}, u32[]{:S(2)}, u32[]{:S(2)}) collective-permute-start(bf16[28,8,48]{2,1,0:T(8,128)(2,1)S(1)} %get-tuple-element.14), channel_id=1, source_target_pairs={{0,1},{2,3},{4,5},{6,7},{8,9},{10,11},{12,13},{14,15},{16,17},{18,... | collective-permute-start | bytes 64520 | tf_op jit(solution)/shard_map/ppermute | solution.py:17
  60.5 3.1 %collective-permute-start.7 = (bf16[28,8,48]{2,1,0:T(8,128)(2,1)S(1)}, bf16[28,8,48]{2,1,0:T(8,128)(2,1)S(1)}, u32[]{:S(2)}, u32[]{:S(2)}) collective-permute-start(bf16[28,8,48]{2,1,0:T(8,128)(2,1)S(1)} %get-tuple-element.15), channel_id=1, source_target_pairs={{1,0},{3,2},{5,4},{7,6},{9,8},{11,10},{13,12},{15,14},{17,16},{19,... | collective-permute-start | bytes 64520 | tf_op jit(solution)/shard_map/ppermute | solution.py:18
  64.0 0.9 copy-start.2
  64.6 0.7 copy-start.7
  66.6 12.8 %all-to-all-start = ((bf16[8,2,1728]{2,1,0:T(2,128)(2,1)}), bf16[8,2,1728]{2,1,0:T(2,128)(2,1)S(1)}, u32[]{:S(2)}, u32[]{:S(2)}) async-start(bf16[8,2,1728]{2,1,0:T(2,128)(2,1)} %reshape.35), calls=%async_computation | async-start | bytes 114688 | tf_op jit(solution)/shard_map/all_to_all | solution.py:100
  84.1 6.6 %collective-permute-start.8 = (bf16[4,6,12,48]{3,0,2,1:T(4,128)(2,1)S(1)}, bf16[4,6,12,48]{3,0,2,1:T(4,128)(2,1)S(1)}, u32[]{:S(2)}, u32[]{:S(2)}) collective-permute-start(bf16[4,6,12,48]{3,0,2,1:T(4,128)(2,1)S(1)} %get-tuple-element.28), channel_id=1, source_target_pairs={{0,8},{2,10},{4,12},{6,14},{8,0},{10,2},{12,4},{14,6},{1,9},{3,11}... | collective-permute-start | bytes 82952 | tf_op jit(solution)/shard_map/ppermute | solution.py:26
  91.0 0.7 copy-start.8
  91.0 0.7 copy-start.9
  91.0 0.7 copy-start.10
where the time goes:
time: 93.2 us; the launch traced here: 92.6 us
  blocking collectives  36.1 us (39%)
  waiting for transfers between devices  26.4 us (28%)
  starting transfers between devices  20.5 us (22%)
  local copies, waits for them, and re-layouts  7.02 us (8%)
  matrix products  1.8 us (2%)
    all_gather x1, blocking collectives, on_device(): all_bins = lax.all_gather(embedding, 'row', axis=0, tiled=True)  32.3 us
    ppermute x4, waiting for transfers between devices, padded(): after = lax.ppermute(leading, axis, down)  12 us
    ppermute x4, starting transfers between devices, padded(): before = lax.ppermute(last, axis, up)  8.8 us
    all_to_all x1, waiting for transfers between devices, on_device(): lax.all_to_all(arranged, 'row', split_axis=0, concat_axis=0, tiled=True)  6.85 us
    ppermute x1, waiting for transfers between devices, swapped(): return lax.ppermute(value, axis, pairs)  6.02 us
    all_to_all x1, starting transfers between devices, on_device(): lax.all_to_all(arranged, 'row', split_axis=0, concat_axis=0, tiled=True)  5.98 us
    ppermute x4, starting transfers between devices, padded(): after = lax.ppermute(leading, axis, down)  5.17 us
    unnamed x27, local copies, waits for them, and re-layouts  4.82 us
  transfers between devices with their start and end apart: 10, of which 8 were waited for; matrix products, arithmetic and copies ran while one was open for 0% of the time, Pallas kernels for 0%

commit v1 on v0

--- a/solution.py
+++ b/solution.py
@@ -5,6 +5,28 @@
 
 FIRST_DILATION = 4
 SECOND_DILATION = 8
+
+
+def laid_out(blocks, dim):
+    lengths = list(blocks.shape[1:])
+    lengths[dim] *= blocks.shape[0]
+    return jnp.moveaxis(blocks, 0, dim).reshape(lengths)
+
+
+def gather_around(value, axis, dim):
+    size = lax.axis_size(axis)
+    pairs = [(i, (i + 1) % size) for i in range(size)]
+    back = [(b, a) for a, b in pairs]
+    lower, upper = ([], [])
+    for lap in range(size - 1):
+        if lap % 2 == 0:
+            lower.append(lax.ppermute(lower[-1] if lower else value, axis, pairs))
+        else:
+            upper.append(lax.ppermute(upper[-1] if upper else value, axis, back))
+    pieces = jnp.stack([*lower[::-1], value, *upper])
+    shift = lax.axis_index(axis) - len(lower)
+    pieces = pieces[(jnp.arange(size) - shift) % size]
+    return laid_out(pieces, dim)
 
 
 def padded(array, sides, width):
@@ -58,7 +80,7 @@
     row_count = lax.axis_size("row")
     row_at = lax.axis_index("row")
     col_at = lax.axis_index("col")
-    all_bins = lax.all_gather(embedding, "row", axis=0, tiled=True)
+    all_bins = gather_around(embedding, "row", 0)
     row_terms = jnp.dot(all_bins, w_row, preferred_element_type=jnp.float32)
     col_terms = jnp.dot(all_bins, w_col, preferred_element_type=jnp.float32)
     own_rows = lax.dynamic_slice_in_dim(row_terms, row_at * patch_rows, patch_rows, 0)

time: 93.2 us -> 89.2 us (0.957)
  blocking collectives: 36.1 us -> 3.77 us
  starting transfers between devices: 20.5 us -> 39.7 us
  waiting for transfers between devices: 26.4 us -> 34.7 us
    all_gather x1 -> x0, blocking collectives: 32.3 us -> none  [on_device(): all_bins = lax.all_gather(embedding, 'row', axis=0, tiled=True)]
    ppermute x0 -> x7, starting transfers between devices: none -> 17.5 us  [the longest x3 14.5 us: gather_around(): upper.append(lax.ppermute(upper[-1] if upper else value, axis, back))]
    ppermute x0 -> x7, waiting for transfers between devices: none -> 9.16 us  [the longest x4 9.15 us: gather_around(): lower.append(lax.ppermute(lower[-1] if lower else value, axis, pairs))]
    all_to_all x1, starting transfers between devices: 5.98 us -> 9.31 us  [on_device(): lax.all_to_all(arranged, 'row', split_axis=0, concat_axis=0, tiled=True)]
    ppermute x4, waiting for transfers between devices: 12 us -> 10.2 us  [padded(): after = lax.ppermute(leading, axis, down)]
    ppermute x4, starting transfers between devices: 8.8 us -> 7.21 us  [padded(): before = lax.ppermute(last, axis, up)]
    ppermute x4, waiting for transfers between devices: 1.5 us -> 2.49 us  [padded(): before = lax.ppermute(last, axis, up)]
    unnamed x27 -> x33, local copies, waits for them, and re-layouts: 4.82 us -> 4.82 us
  transfers between devices with their start and end apart: 10 -> 17, of which waited for: 8 -> 12; matrix products, arithmetic and copies ran while one was open for 0% -> 0% of each run, Pallas kernels for 0% -> 0%
where the time goes in v1:
time: 89.2 us; the launch traced here: 88.5 us
  starting transfers between devices  39.7 us (45%)
  waiting for transfers between devices  34.7 us (39%)
  local copies, waits for them, and re-layouts  7.61 us (9%)
  blocking collectives  3.77 us (4%)
  matrix products  1.8 us (2%)
    ppermute x3, starting transfers between devices, gather_around(): upper.append(lax.ppermute(upper[-1] if upper else value, axis, back))  14.5 us
    ppermute x4, waiting for transfers between devices, padded(): after = lax.ppermute(leading, axis, down)  10.2 us
    all_to_all x1, starting transfers between devices, on_device(): lax.all_to_all(arranged, 'row', split_axis=0, concat_axis=0, tiled=True)  9.31 us
    ppermute x4, waiting for transfers between devices, gather_around(): lower.append(lax.ppermute(lower[-1] if lower else value, axis, pairs))  9.15 us
    ppermute x4, starting transfers between devices, padded(): before = lax.ppermute(last, axis, up)  7.21 us
    all_to_all x1, waiting for transfers between devices, on_device(): lax.all_to_all(arranged, 'row', split_axis=0, concat_axis=0, tiled=True)  6.85 us
    ppermute x1, waiting for transfers between devices, swapped(): return lax.ppermute(value, axis, pairs)  6.02 us
    ppermute x4, starting transfers between devices, padded(): after = lax.ppermute(leading, axis, down)  5.17 us
  transfers between devices with their start and end apart: 17, of which 12 were waited for; matrix products, arithmetic and copies ran while one was open for 0% of the time, Pallas kernels for 0%

profile of v1, /device:TPU:0, one launch (start us, length us, event | category | flops | bytes accessed | tf_op | source)
XLA Modules:
  0.0 88.5 jit_solution(2456109189478514759)
XLA Ops:
  0.0 2.9 %collective-permute-start = (bf16[12,96]{1,0:T(8,128)(2,1)}, bf16[12,96]{1,0:T(8,128)(2,1)S(1)}, u32[]{:S(2)}, u32[]{:S(2)}) collective-permute-start(bf16[12,96]{1,0:T(8,128)(2,1)} %param.12), channel_id=1, source_target_pairs={{0,2},{2,4},{4,6},{6,8},{8,10},{10,12},{12,14},{14,0},{1,3},{3,5},... | collective-permute-start | bytes 6920 | tf_op jit(solution)/shard_map/ppermute | solution.py:23
  2.9 4.8 %collective-permute-done = bf16[12,96]{1,0:T(8,128)(2,1)S(1)} collective-permute-done((bf16[12,96]{1,0:T(8,128)(2,1)}, bf16[12,96]{1,0:T(8,128)(2,1)S(1)}, u32[]{:S(2)}, u32[]{:S(2)}) %collective-permute-start) | collective-permute-done | bytes 2336 | tf_op jit(solution)/shard_map/ppermute | solution.py:23
  7.8 4.7 %collective-permute-start.4 = (bf16[12,96]{1,0:T(8,128)(2,1)}, bf16[12,96]{1,0:T(8,128)(2,1)S(1)}, u32[]{:S(2)}, u32[]{:S(2)}) collective-permute-start(bf16[12,96]{1,0:T(8,128)(2,1)} %param.12), channel_id=1, source_target_pairs={{2,0},{4,2},{6,4},{8,6},{10,8},{12,10},{14,12},{0,14},{3,1},{5,3},... | collective-permute-start | bytes 6920 | tf_op jit(solution)/shard_map/ppermute | solution.py:25
  12.5 1.6 %collective-permute-done.1 = bf16[12,96]{1,0:T(8,128)(2,1)S(1)} collective-permute-done((bf16[12,96]{1,0:T(8,128)(2,1)S(1)}, bf16[12,96]{1,0:T(8,128)(2,1)S(1)}, u32[]{:S(2)}, u32[]{:S(2)}) %collective-permute-start.1) | collective-permute-done | bytes 2336 | tf_op jit(solution)/shard_map/ppermute | solution.py:23
  14.1 4.9 %collective-permute-start.5 = (bf16[12,96]{1,0:T(8,128)(2,1)S(1)}, bf16[12,96]{1,0:T(8,128)(2,1)S(1)}, u32[]{:S(2)}, u32[]{:S(2)}) collective-permute-start(bf16[12,96]{1,0:T(8,128)(2,1)S(1)} %collective-permute-done.4), channel_id=1, source_target_pairs={{2,0},{4,2},{6,4},{8,6},{10,8},{12,10},{14,12},{0,14},{3,1},{5,3},... | collective-permute-start | bytes 6920 | tf_op jit(solution)/shard_map/ppermute | solution.py:25
  19.0 1.4 %collective-permute-done.2 = bf16[12,96]{1,0:T(8,128)(2,1)S(1)} collective-permute-done((bf16[12,96]{1,0:T(8,128)(2,1)S(1)}, bf16[12,96]{1,0:T(8,128)(2,1)S(1)}, u32[]{:S(2)}, u32[]{:S(2)}) %collective-permute-start.2) | collective-permute-done | bytes 2336 | tf_op jit(solution)/shard_map/ppermute | solution.py:23
  20.4 4.9 %collective-permute-start.6 = (bf16[12,96]{1,0:T(8,128)(2,1)S(1)}, bf16[12,96]{1,0:T(8,128)(2,1)S(1)}, u32[]{:S(2)}, u32[]{:S(2)}) collective-permute-start(bf16[12,96]{1,0:T(8,128)(2,1)S(1)} %collective-permute-done.5), channel_id=1, source_target_pairs={{2,0},{4,2},{6,4},{8,6},{10,8},{12,10},{14,12},{0,14},{3,1},{5,3},... | collective-permute-start | bytes 6920 | tf_op jit(solution)/shard_map/ppermute | solution.py:25
  25.3 1.4 %collective-permute-done.3 = bf16[12,96]{1,0:T(8,128)(2,1)S(1)} collective-permute-done((bf16[12,96]{1,0:T(8,128)(2,1)S(1)}, bf16[12,96]{1,0:T(8,128)(2,1)S(1)}, u32[]{:S(2)}, u32[]{:S(2)}) %collective-permute-start.3) | collective-permute-done | bytes 2336 | tf_op jit(solution)/shard_map/ppermute | solution.py:23
  29.0 1.3 %collective-permute-start.7 = (bf16[4,48,48]{2,1,0:T(8,128)(2,1)S(1)}, bf16[4,48,48]{2,1,0:T(8,128)(2,1)S(1)}, u32[]{:S(2)}, u32[]{:S(2)}) collective-permute-start(bf16[4,48,48]{2,1,0:T(8,128)(2,1)S(1)} %get-tuple-element.31), channel_id=1, source_target_pairs={{0,2},{2,4},{4,6},{6,8},{8,10},{10,12},{12,14},{1,3},{3,5},{5,7},{... | collective-permute-start | bytes 55304 | tf_op jit(solution)/shard_map/ppermute | solution.py:39
  30.3 1.3 %collective-permute-start.8 = (bf16[4,48,48]{2,1,0:T(8,128)(2,1)S(1)}, bf16[4,48,48]{2,1,0:T(8,128)(2,1)S(1)}, u32[]{:S(2)}, u32[]{:S(2)}) collective-permute-start(bf16[4,48,48]{2,1,0:T(8,128)(2,1)S(1)} %get-tuple-element.32), channel_id=1, source_target_pairs={{2,0},{4,2},{6,4},{8,6},{10,8},{12,10},{14,12},{3,1},{5,3},{7,5},{... | collective-permute-start | bytes 55304 | tf_op jit(solution)/shard_map/ppermute | solution.py:40
  32.0 4.3 %collective-permute-done.8 = bf16[4,48,48]{2,1,0:T(8,128)(2,1)S(1)} collective-permute-done((bf16[4,48,48]{2,1,0:T(8,128)(2,1)S(1)}, bf16[4,48,48]{2,1,0:T(8,128)(2,1)S(1)}, u32[]{:S(2)}, u32[]{:S(2)}) %collective-permute-start.8) | collective-permute-done | bytes 18464 | tf_op jit(solution)/shard_map/ppermute | solution.py:40
  36.3 1.3 %collective-permute-start.10 = (bf16[20,4,48]{2,1,0:T(4,128)(2,1)S(1)}, bf16[20,4,48]{2,1,0:T(4,128)(2,1)S(1)}, u32[]{:S(2)}, u32[]{:S(2)}) collective-permute-start(bf16[20,4,48]{2,1,0:T(4,128)(2,1)S(1)} %get-tuple-element.26), channel_id=1, source_target_pairs={{1,0},{3,2},{5,4},{7,6},{9,8},{11,10},{13,12},{15,14},{17,16},{19,... | collective-permute-start | bytes 23048 | tf_op jit(solution)/shard_map/ppermute | solution.py:40
  37.6 3.0 %collective-permute-start.9 = (bf16[20,4,48]{2,1,0:T(4,128)(2,1)S(1)}, bf16[20,4,48]{2,1,0:T(4,128)(2,1)S(1)}, u32[]{:S(2)}, u32[]{:S(2)}) collective-permute-start(bf16[20,4,48]{2,1,0:T(4,128)(2,1)S(1)} %get-tuple-element.25), channel_id=1, source_target_pairs={{0,1},{2,3},{4,5},{6,7},{8,9},{10,11},{12,13},{14,15},{16,17},{18,... | collective-permute-start | bytes 23048 | tf_op jit(solution)/shard_map/ppermute | solution.py:39
  43.5 1.6 %collective-permute-start.11 = (bf16[8,48,48]{2,1,0:T(8,128)(2,1)S(1)}, bf16[8,48,48]{2,1,0:T(8,128)(2,1)S(1)}, u32[]{:S(2)}, u32[]{:S(2)}) collective-permute-start(bf16[8,48,48]{2,1,0:T(8,128)(2,1)S(1)} %get-tuple-element.29), channel_id=1, source_target_pairs={{0,2},{2,4},{4,6},{6,8},{8,10},{10,12},{12,14},{1,3},{3,5},{5,7},{... | collective-permute-start | bytes 110600 | tf_op jit(solution)/shard_map/ppermute | solution.py:39
  45.1 1.3 %collective-permute-start.12 = (bf16[8,48,48]{2,1,0:T(8,128)(2,1)S(1)}, bf16[8,48,48]{2,1,0:T(8,128)(2,1)S(1)}, u32[]{:S(2)}, u32[]{:S(2)}) collective-permute-start(bf16[8,48,48]{2,1,0:T(8,128)(2,1)S(1)} %get-tuple-element.30), channel_id=1, source_target_pairs={{2,0},{4,2},{6,4},{8,6},{10,8},{12,10},{14,12},{3,1},{5,3},{7,5},{... | collective-permute-start | bytes 110600 | tf_op jit(solution)/shard_map/ppermute | solution.py:40
  46.4 1.2 %collective-permute-done.11 = bf16[8,48,48]{2,1,0:T(8,128)(2,1)S(1)} collective-permute-done((bf16[8,48,48]{2,1,0:T(8,128)(2,1)S(1)}, bf16[8,48,48]{2,1,0:T(8,128)(2,1)S(1)}, u32[]{:S(2)}, u32[]{:S(2)}) %collective-permute-start.11) | collective-permute-done | bytes 36896 | tf_op jit(solution)/shard_map/ppermute | solution.py:39
  47.6 4.1 %collective-permute-done.12 = bf16[8,48,48]{2,1,0:T(8,128)(2,1)S(1)} collective-permute-done((bf16[8,48,48]{2,1,0:T(8,128)(2,1)S(1)}, bf16[8,48,48]{2,1,0:T(8,128)(2,1)S(1)}, u32[]{:S(2)}, u32[]{:S(2)}) %collective-permute-start.12) | collective-permute-done | bytes 36896 | tf_op jit(solution)/shard_map/ppermute | solution.py:40
  51.8 1.3 %collective-permute-start.13 = (bf16[28,8,48]{2,1,0:T(8,128)(2,1)S(1)}, bf16[28,8,48]{2,1,0:T(8,128)(2,1)S(1)}, u32[]{:S(2)}, u32[]{:S(2)}) collective-permute-start(bf16[28,8,48]{2,1,0:T(8,128)(2,1)S(1)} %get-tuple-element.14), channel_id=1, source_target_pairs={{0,1},{2,3},{4,5},{6,7},{8,9},{10,11},{12,13},{14,15},{16,17},{18,... | collective-permute-start | bytes 64520 | tf_op jit(solution)/shard_map/ppermute | solution.py:39
  53.1 1.3 %collective-permute-start.14 = (bf16[28,8,48]{2,1,0:T(8,128)(2,1)S(1)}, bf16[28,8,48]{2,1,0:T(8,128)(2,1)S(1)}, u32[]{:S(2)}, u32[]{:S(2)}) collective-permute-start(bf16[28,8,48]{2,1,0:T(8,128)(2,1)S(1)} %get-tuple-element.15), channel_id=1, source_target_pairs={{1,0},{3,2},{5,4},{7,6},{9,8},{11,10},{13,12},{15,14},{17,16},{19,... | collective-permute-start | bytes 64520 | tf_op jit(solution)/shard_map/ppermute | solution.py:40
  54.4 1.8 %collective-permute-done.14 = bf16[28,8,48]{2,1,0:T(8,128)(2,1)S(1)} collective-permute-done((bf16[28,8,48]{2,1,0:T(8,128)(2,1)S(1)}, bf16[28,8,48]{2,1,0:T(8,128)(2,1)S(1)}, u32[]{:S(2)}, u32[]{:S(2)}) %collective-permute-start.14) | collective-permute-done | bytes 21536 | tf_op jit(solution)/shard_map/ppermute | solution.py:40
  59.2 9.3 %all-to-all-start = ((bf16[8,2,1728]{2,1,0:T(2,128)(2,1)}), bf16[8,2,1728]{2,1,0:T(2,128)(2,1)S(1)}, u32[]{:S(2)}, u32[]{:S(2)}) async-start(bf16[8,2,1728]{2,1,0:T(2,128)(2,1)} %reshape.94), calls=%async_computation | async-start | bytes 114688 | tf_op jit(solution)/shard_map/all_to_all | solution.py:122
  68.5 6.8 %all-to-all-done = bf16[8,2,1728]{2,1,0:T(2,128)(2,1)S(1)} async-done(((bf16[8,2,1728]{2,1,0:T(2,128)(2,1)}), bf16[8,2,1728]{2,1,0:T(2,128)(2,1)S(1)}, u32[]{:S(2)}, u32[]{:S(2)}) %all-to-all-start) | async-done | bytes 55328 | tf_op jit(solution)/shard_map/all_to_all | solution.py:122
  75.8 3.8 %all_to_all.10 = bf16[2,2,6912]{2,1,0:T(2,128)(2,1)S(1)} all-to-all(bf16[2,2,6912]{2,1,0:T(2,128)(2,1)S(1)} %reshape.96), channel_id=1, replica_groups=mesh['group'=2,'row'=8,'col'=2] {'col'}, dimensions={0} | all-to-all | bytes 110592 | tf_op jit(solution)/shard_map/all_to_all | solution.py:121
  80.5 6.0 %collective-permute-done.15 = bf16[4,6,12,48]{3,0,2,1:T(4,128)(2,1)S(1)} collective-permute-done((bf16[4,6,12,48]{3,0,2,1:T(4,128)(2,1)S(1)}, bf16[4,6,12,48]{3,0,2,1:T(4,128)(2,1)S(1)}, u32[]{:S(2)}, u32[]{:S(2)}) %collective-permute-start.15) | collective-permute-done | bytes 27680 | tf_op jit(solution)/shard_map/ppermute | solution.py:48
  (75 shorter events, 11.8 us)
Async XLA Ops:
  0.0 42.5 %copy-start = (bf16[3,3,48,48]{3,2,1,0:T(8,128)(2,1)S(1)}, bf16[3,3,48,48]{3,2,1,0:T(8,128)(2,1)}, u32[]{:S(2)}) copy-start(bf16[3,3,48,48]{3,2,1,0:T(8,128)(2,1)} %param.15) | copy-start | bytes 124420
  0.0 7.8 %collective-permute-start = (bf16[12,96]{1,0:T(8,128)(2,1)}, bf16[12,96]{1,0:T(8,128)(2,1)S(1)}, u32[]{:S(2)}, u32[]{:S(2)}) collective-permute-start(bf16[12,96]{1,0:T(8,128)(2,1)} %param.12), channel_id=1, source_target_pairs={{0,2},{2,4},{4,6},{6,8},{8,10},{10,12},{12,14},{14,0},{1,3},{3,5},... | collective-permute-start | bytes 6920 | tf_op jit(solution)/shard_map/ppermute | solution.py:23
  7.8 6.3 %collective-permute-start.1 = (bf16[12,96]{1,0:T(8,128)(2,1)S(1)}, bf16[12,96]{1,0:T(8,128)(2,1)S(1)}, u32[]{:S(2)}, u32[]{:S(2)}) collective-permute-start(bf16[12,96]{1,0:T(8,128)(2,1)S(1)} %collective-permute-done), channel_id=1, source_target_pairs={{0,2},{2,4},{4,6},{6,8},{8,10},{10,12},{12,14},{14,0},{1,3},{3,5},... | collective-permute-start | bytes 6920 | tf_op jit(solution)/shard_map/ppermute | solution.py:23
  7.8 6.3 %collective-permute-start.4 = (bf16[12,96]{1,0:T(8,128)(2,1)}, bf16[12,96]{1,0:T(8,128)(2,1)S(1)}, u32[]{:S(2)}, u32[]{:S(2)}) collective-permute-start(bf16[12,96]{1,0:T(8,128)(2,1)} %param.12), channel_id=1, source_target_pairs={{2,0},{4,2},{6,4},{8,6},{10,8},{12,10},{14,12},{0,14},{3,1},{5,3},... | collective-permute-start | bytes 6920 | tf_op jit(solution)/shard_map/ppermute | solution.py:25
  14.1 6.3 %collective-permute-start.2 = (bf16[12,96]{1,0:T(8,128)(2,1)S(1)}, bf16[12,96]{1,0:T(8,128)(2,1)S(1)}, u32[]{:S(2)}, u32[]{:S(2)}) collective-permute-start(bf16[12,96]{1,0:T(8,128)(2,1)S(1)} %collective-permute-done.1), channel_id=1, source_target_pairs={{0,2},{2,4},{4,6},{6,8},{8,10},{10,12},{12,14},{14,0},{1,3},{3,5},... | collective-permute-start | bytes 6920 | tf_op jit(solution)/shard_map/ppermute | solution.py:23
  14.1 6.3 %collective-permute-start.5 = (bf16[12,96]{1,0:T(8,128)(2,1)S(1)}, bf16[12,96]{1,0:T(8,128)(2,1)S(1)}, u32[]{:S(2)}, u32[]{:S(2)}) collective-permute-start(bf16[12,96]{1,0:T(8,128)(2,1)S(1)} %collective-permute-done.4), channel_id=1, source_target_pairs={{2,0},{4,2},{6,4},{8,6},{10,8},{12,10},{14,12},{0,14},{3,1},{5,3},... | collective-permute-start | bytes 6920 | tf_op jit(solution)/shard_map/ppermute | solution.py:25
  20.4 6.3 %collective-permute-start.3 = (bf16[12,96]{1,0:T(8,128)(2,1)S(1)}, bf16[12,96]{1,0:T(8,128)(2,1)S(1)}, u32[]{:S(2)}, u32[]{:S(2)}) collective-permute-start(bf16[12,96]{1,0:T(8,128)(2,1)S(1)} %collective-permute-done.2), channel_id=1, source_target_pairs={{0,2},{2,4},{4,6},{6,8},{8,10},{10,12},{12,14},{14,0},{1,3},{3,5},... | collective-permute-start | bytes 6920 | tf_op jit(solution)/shard_map/ppermute | solution.py:23
  20.4 7.0 %collective-permute-start.6 = (bf16[12,96]{1,0:T(8,128)(2,1)S(1)}, bf16[12,96]{1,0:T(8,128)(2,1)S(1)}, u32[]{:S(2)}, u32[]{:S(2)}) collective-permute-start(bf16[12,96]{1,0:T(8,128)(2,1)S(1)} %collective-permute-done.5), channel_id=1, source_target_pairs={{2,0},{4,2},{6,4},{8,6},{10,8},{12,10},{14,12},{0,14},{3,1},{5,3},... | collective-permute-start | bytes 6920 | tf_op jit(solution)/shard_map/ppermute | solution.py:25
  27.4 0.7 copy-start.3
  27.4 0.8 copy-start.4
  28.0 0.9 %copy-start.1 = (bf16[12,48,48]{2,1,0:T(8,128)(2,1)S(1)}, bf16[12,48,48]{2,1,0:T(8,128)(2,1)}, u32[]{:S(2)}) copy-start(bf16[12,48,48]{2,1,0:T(8,128)(2,1)} %param.11) | copy-start | bytes 165892
  29.0 3.0 %collective-permute-start.7 = (bf16[4,48,48]{2,1,0:T(8,128)(2,1)S(1)}, bf16[4,48,48]{2,1,0:T(8,128)(2,1)S(1)}, u32[]{:S(2)}, u32[]{:S(2)}) collective-permute-start(bf16[4,48,48]{2,1,0:T(8,128)(2,1)S(1)} %get-tuple-element.31), channel_id=1, source_target_pairs={{0,2},{2,4},{4,6},{6,8},{8,10},{10,12},{12,14},{1,3},{3,5},{5,7},{... | collective-permute-start | bytes 55304 | tf_op jit(solution)/shard_map/ppermute | solution.py:39
  30.3 6.0 %collective-permute-start.8 = (bf16[4,48,48]{2,1,0:T(8,128)(2,1)S(1)}, bf16[4,48,48]{2,1,0:T(8,128)(2,1)S(1)}, u32[]{:S(2)}, u32[]{:S(2)}) collective-permute-start(bf16[4,48,48]{2,1,0:T(8,128)(2,1)S(1)} %get-tuple-element.32), channel_id=1, source_target_pairs={{2,0},{4,2},{6,4},{8,6},{10,8},{12,10},{14,12},{3,1},{5,3},{7,5},{... | collective-permute-start | bytes 55304 | tf_op jit(solution)/shard_map/ppermute | solution.py:40
  36.3 4.3 %collective-permute-start.10 = (bf16[20,4,48]{2,1,0:T(4,128)(2,1)S(1)}, bf16[20,4,48]{2,1,0:T(4,128)(2,1)S(1)}, u32[]{:S(2)}, u32[]{:S(2)}) collective-permute-start(bf16[20,4,48]{2,1,0:T(4,128)(2,1)S(1)} %get-tuple-element.26), channel_id=1, source_target_pairs={{1,0},{3,2},{5,4},{7,6},{9,8},{11,10},{13,12},{15,14},{17,16},{19,... | collective-permute-start | bytes 23048 | tf_op jit(solution)/shard_map/ppermute | solution.py:40
  37.6 3.9 %collective-permute-start.9 = (bf16[20,4,48]{2,1,0:T(4,128)(2,1)S(1)}, bf16[20,4,48]{2,1,0:T(4,128)(2,1)S(1)}, u32[]{:S(2)}, u32[]{:S(2)}) collective-permute-start(bf16[20,4,48]{2,1,0:T(4,128)(2,1)S(1)} %get-tuple-element.25), channel_id=1, source_target_pairs={{0,1},{2,3},{4,5},{6,7},{8,9},{10,11},{12,13},{14,15},{16,17},{18,... | collective-permute-start | bytes 23048 | tf_op jit(solution)/shard_map/ppermute | solution.py:39
  43.5 4.1 %collective-permute-start.11 = (bf16[8,48,48]{2,1,0:T(8,128)(2,1)S(1)}, bf16[8,48,48]{2,1,0:T(8,128)(2,1)S(1)}, u32[]{:S(2)}, u32[]{:S(2)}) collective-permute-start(bf16[8,48,48]{2,1,0:T(8,128)(2,1)S(1)} %get-tuple-element.29), channel_id=1, source_target_pairs={{0,2},{2,4},{4,6},{6,8},{8,10},{10,12},{12,14},{1,3},{3,5},{5,7},{... | collective-permute-start | bytes 110600 | tf_op jit(solution)/shard_map/ppermute | solution.py:39
  45.1 6.7 %collective-permute-start.12 = (bf16[8,48,48]{2,1,0:T(8,128)(2,1)S(1)}, bf16[8,48,48]{2,1,0:T(8,128)(2,1)S(1)}, u32[]{:S(2)}, u32[]{:S(2)}) collective-permute-start(bf16[8,48,48]{2,1,0:T(8,128)(2,1)S(1)} %get-tuple-element.30), channel_id=1, source_target_pairs={{2,0},{4,2},{6,4},{8,6},{10,8},{12,10},{14,12},{3,1},{5,3},{7,5},{... | collective-permute-start | bytes 110600 | tf_op jit(solution)/shard_map/ppermute | solution.py:40
  51.8 2.6 %collective-permute-start.13 = (bf16[28,8,48]{2,1,0:T(8,128)(2,1)S(1)}, bf16[28,8,48]{2,1,0:T(8,128)(2,1)S(1)}, u32[]{:S(2)}, u32[]{:S(2)}) collective-permute-start(bf16[28,8,48]{2,1,0:T(8,128)(2,1)S(1)} %get-tuple-element.14), channel_id=1, source_target_pairs={{0,1},{2,3},{4,5},{6,7},{8,9},{10,11},{12,13},{14,15},{16,17},{18,... | collective-permute-start | bytes 64520 | tf_op jit(solution)/shard_map/ppermute | solution.py:39
  53.1 3.1 %collective-permute-start.14 = (bf16[28,8,48]{2,1,0:T(8,128)(2,1)S(1)}, bf16[28,8,48]{2,1,0:T(8,128)(2,1)S(1)}, u32[]{:S(2)}, u32[]{:S(2)}) collective-permute-start(bf16[28,8,48]{2,1,0:T(8,128)(2,1)S(1)} %get-tuple-element.15), channel_id=1, source_target_pairs={{1,0},{3,2},{5,4},{7,6},{9,8},{11,10},{13,12},{15,14},{17,16},{19,... | collective-permute-start | bytes 64520 | tf_op jit(solution)/shard_map/ppermute | solution.py:40
  56.5 0.9 %copy-start.2 = (bf16[3,3,48,48]{3,2,1,0:T(8,128)(2,1)S(1)}, bf16[3,3,48,48]{3,2,1,0:T(8,128)(2,1)}, u32[]{:S(2)}) copy-start(bf16[3,3,48,48]{3,2,1,0:T(8,128)(2,1)} %param.17) | copy-start | bytes 124420
  59.2 16.2 %all-to-all-start = ((bf16[8,2,1728]{2,1,0:T(2,128)(2,1)}), bf16[8,2,1728]{2,1,0:T(2,128)(2,1)S(1)}, u32[]{:S(2)}, u32[]{:S(2)}) async-start(bf16[8,2,1728]{2,1,0:T(2,128)(2,1)} %reshape.94), calls=%async_computation | async-start | bytes 114688 | tf_op jit(solution)/shard_map/all_to_all | solution.py:122
  80.0 6.6 %collective-permute-start.15 = (bf16[4,6,12,48]{3,0,2,1:T(4,128)(2,1)S(1)}, bf16[4,6,12,48]{3,0,2,1:T(4,128)(2,1)S(1)}, u32[]{:S(2)}, u32[]{:S(2)}) collective-permute-start(bf16[4,6,12,48]{3,0,2,1:T(4,128)(2,1)S(1)} %get-tuple-element.28), channel_id=1, source_target_pairs={{0,8},{2,10},{4,12},{6,14},{8,0},{10,2},{12,4},{14,6},{1,9},{3,11}... | collective-permute-start | bytes 82952 | tf_op jit(solution)/shard_map/ppermute | solution.py:48
  86.9 0.7 copy-start.8
  86.9 0.7 copy-start.9
  (4 other events, 2.7 us)
